TPU v7x, 256 devices: a whole 4x4x8 slice. The times are simulated.
256 devices in a mesh: req: 32 (over y, x, core), head: 8 (over z).
Axes of the slice: x: 4, y: 4, z: 8, core: 2. Of those that a mesh axis runs over, the one named last changes fastest.
Arguments:
- queries: bfloat16 [1024, 16384], P(('req', 'head')), may hold values from -15 to 15
- cache_keys: bfloat16 [8, 32768, 1024], P(None, 'req', 'head'), may hold values from -6 to 6
- cache_values: bfloat16 [8, 32768, 1024], P(None, 'req', 'head'), may hold values from -6 to 6
- tree_keys: bfloat16 [1024, 1024], P('req', 'head'), may hold values from -10 to 10
- tree_values: bfloat16 [1024, 1024], P('req', 'head'), may hold values from -6 to 6
- parents: int32 [8, 128], replicated, may hold values from -1 to 126, as said below
- tree_sizes: int32 [8], replicated, may hold values from 16 to 128
- cache_lens: int32 [8], replicated, may hold values from 2 to 32768
Outputs:
- attended: bfloat16 [1024, 16384], P('req', 'head')
Inputs may be any that keep to these rules, and one draw needn't show every extreme that they name: parents[a, 0] = -1 (the root); for node i >= 1, parents[a, i] is a node of 0 to i - 1.
All inputs are finite; a program needn't handle non-finite values.
Results may differ from a plain program's by a relative error of at most 0.003.
Values may be sent and summed in bfloat16 or wider, within the bound.
A program may use at most 128 MiB of HBM per device.

v0:
```python
import math
import jax
import jax.numpy as jnp
from jax import lax
from jax.sharding import Mesh
from jax.sharding import PartitionSpec as P

NH = 128
KVH = 8
HD = 128
negative_fill = -1e30


def ancestry(parents):
    node_count = parents.shape[1]
    node_ids = jnp.arange(node_count, dtype=jnp.int32)
    linked = jnp.logical_or(
        parents[:, :, None] == node_ids[None, None, :], node_ids[:, None] == node_ids[None, :]
    )
    reached = linked.astype(jnp.bfloat16)
    for doubling in range((node_count - 1).bit_length()):
        squared = jnp.einsum("aij,ajk->aik", reached, reached, preferred_element_type=jnp.float32)
        reached = jnp.minimum(squared, 1.0).astype(jnp.bfloat16)
    return reached


def body(
    queries, cache_keys, cache_values, tree_keys, tree_values, parents, tree_sizes, cache_lens
):
    group_size = NH // KVH
    softmax_scale = 1.0 / math.sqrt(HD)
    request = lax.axis_index("rh")
    quarter = lax.axis_index("rl")
    n_lo = lax.axis_size("rl")
    n_hi = lax.axis_size("rh")
    cache_block = cache_keys.shape[1]
    kv_local = cache_keys.shape[2] // HD
    heads_local = kv_local * group_size
    node_count = parents.shape[1]
    rows_owned = tree_keys.shape[0]
    by_head = lax.all_to_all(queries, "head", split_axis=1, concat_axis=0, tiled=True)
    query_block = lax.all_gather(by_head, "rl", axis=0, tiled=True)
    query_block = query_block.reshape(node_count, kv_local, group_size, HD)
    both = jnp.concatenate([cache_keys, cache_values], axis=2)
    mine = lax.all_to_all(both, "rh", split_axis=0, concat_axis=1, tiled=True)[0]
    mine = mine.reshape(n_hi, cache_block, 2, kv_local, HD)
    reached = ancestry(parents)
    ancestors = lax.dynamic_index_in_dim(reached, request, 0, keepdims=False)
    ancestors = lax.dynamic_slice_in_dim(ancestors, quarter * rows_owned, rows_owned, 1)
    live_tree_all = ancestors > 0.5
    length = lax.dynamic_index_in_dim(cache_lens, request, 0, keepdims=False)
    local_tree_keys = tree_keys.reshape(rows_owned, kv_local, HD)
    local_tree_values = tree_values.reshape(rows_owned, kv_local, HD)

    def one_group(s):
        block = s * n_lo + quarter
        positions = block * cache_block + jnp.arange(cache_block, dtype=jnp.int32)
        live_cache = positions < length
        live_tree = jnp.logical_and(live_tree_all, s == request)
        block_keys = mine[s, :, 0]
        block_values = mine[s, :, 1]
        cache_scores = (
            jnp.einsum(
                "igqd,pgd->igqp", query_block, block_keys, preferred_element_type=jnp.float32
            )
            * softmax_scale
        )
        cache_scores = jnp.where(live_cache[None, None, None, :], cache_scores, negative_fill)
        tree_scores = (
            jnp.einsum(
                "igqd,rgd->igqr", query_block, local_tree_keys, preferred_element_type=jnp.float32
            )
            * softmax_scale
        )
        tree_scores = jnp.where(live_tree[:, None, None, :], tree_scores, negative_fill)
        peaks = jnp.maximum(jnp.max(cache_scores, axis=3), jnp.max(tree_scores, axis=3))
        cache_weights = jnp.where(
            live_cache[None, None, None, :], jnp.exp(cache_scores - peaks[..., None]), 0.0
        )
        tree_weights = jnp.where(
            live_tree[:, None, None, :], jnp.exp(tree_scores - peaks[..., None]), 0.0
        )
        totals = jnp.sum(cache_weights, axis=3) + jnp.sum(tree_weights, axis=3)
        group_sums = jnp.einsum(
            "igqp,pgd->igqd",
            cache_weights.astype(jnp.bfloat16),
            block_values,
            preferred_element_type=jnp.float32,
        )
        group_sums = group_sums + jnp.einsum(
            "igqr,rgd->igqd",
            tree_weights.astype(jnp.bfloat16),
            local_tree_values,
            preferred_element_type=jnp.float32,
        )
        floored = jnp.maximum(totals, 1.0)
        partial_value = group_sums / floored[..., None]
        log_total = peaks + jnp.log(floored)
        return (
            partial_value.reshape(node_count, heads_local, HD),
            log_total.reshape(node_count, heads_local),
        )

    partials, log_totals = lax.map(one_group, jnp.arange(n_hi, dtype=jnp.int32))
    top = jnp.max(log_totals, axis=0)
    weights = jnp.exp(log_totals - top)
    den = jnp.sum(weights, axis=0)
    acc = jnp.sum(weights[..., None] * partials, axis=0)
    payload = jnp.concatenate(
        [acc.reshape(node_count, heads_local * HD), den, top], axis=1
    ).reshape(n_lo, rows_owned, heads_local * HD + 2 * heads_local)
    gathered = lax.all_to_all(payload, "rl", split_axis=0, concat_axis=0, tiled=True)
    got_acc = gathered[:, :, : heads_local * HD].reshape(n_lo, rows_owned, heads_local, HD)
    got_den = gathered[:, :, heads_local * HD : heads_local * HD + heads_local]
    got_top = gathered[:, :, heads_local * HD + heads_local :]
    highest = jnp.max(got_top, axis=0)
    scale = jnp.exp(got_top - highest)
    num = jnp.sum(scale[..., None] * got_acc, axis=0)
    total = jnp.sum(scale * got_den, axis=0)
    merged = (num / total[..., None]).reshape(rows_owned, heads_local * HD)
    row_nodes = quarter * rows_owned + jnp.arange(rows_owned, dtype=jnp.int32)
    live_size = lax.dynamic_index_in_dim(tree_sizes, request, 0, keepdims=False)
    live_rows = row_nodes < live_size
    return jnp.where(live_rows[:, None], merged, 0.0).astype(jnp.bfloat16)


def solution(mesh):

    def run(
        queries, cache_keys, cache_values, tree_keys, tree_values, parents, tree_sizes, cache_lens
    ):
        n_hi = cache_keys.shape[0]
        n_lo = mesh.shape["req"] // n_hi
        split = Mesh(mesh.devices.reshape(n_hi, n_lo, mesh.shape["head"]), ("rh", "rl", "head"))
        rows = ("rh", "rl")
        placed = (
            P(("rh", "rl", "head"), None),
            P(None, rows, "head"),
            P(None, rows, "head"),
            P(rows, "head"),
            P(rows, "head"),
            P(),
            P(),
            P(),
        )
        return jax.shard_map(
            body, mesh=split, in_specs=placed, out_specs=P(rows, "head"), check_vma=False
        )(
            queries,
            cache_keys,
            cache_values,
            tree_keys,
            tree_values,
            parents,
            tree_sizes,
            cache_lens,
        )

    return run
```

profile of v0, /device:TPU:1, one launch (start us, length us, event | category | flops | bytes accessed | tf_op | source)
XLA Modules:
  0.0 273.4 jit_solution(10835699050133776124)
XLA Ops:
  0.0 9.1 %all-to-all-start.1 = ((bf16[4,8,2048]{2,0,1:T(4,128)(2,1)}), bf16[4,8,2048]{2,0,1:T(4,128)(2,1)S(1)}, u32[]{:S(2)}, u32[]{:S(2)}) async-start(bf16[4,8,2048]{2,0,1:T(4,128)(2,1)} %bitcast.168), calls=%async_computation.1 | async-start | bytes 262144 | tf_op jit(solution)/shard_map/all_to_all | solution.py:41
  9.2 2.9 %copy.62 = bf16[8,1024,128]{1,2,0:T(8,128)(2,1)S(1)} copy(bf16[8,1024,128]{2,1,0:T(8,128)(2,1)} %param.12) | data formatting | bytes 4194304 | tf_op args[2]
  12.0 3.9 %copy.61 = bf16[8,1024,128]{1,2,0:T(8,128)(2,1)} copy(bf16[8,1024,128]{2,1,0:T(8,128)(2,1)} %param.11) | data formatting | bytes 4194304 | tf_op args[1]
  16.0 4.2 %pad_maximum_fusion = bf16[8,1024,256]{1,2,0:T(8,128)(2,1)} fusion(bf16[8,1024,128]{1,2,0:T(8,128)(2,1)S(1)} %copy.62, bf16[8,1024,128]{1,2,0:T(8,128)(2,1)} %copy.61), kind=kLoop, calls=%fused_computation.47 | loop fusion | flops 8388608 | bytes 8388608 | tf_op jit(solution)/shard_map/concatenate | solution.py:44
  20.2 6.7 %all-to-all-start = ((bf16[8,1024,256]{1,2,0:T(8,128)(2,1)}), bf16[8,1024,256]{1,2,0:T(8,128)(2,1)}, u32[]{:S(2)}, u32[]{:S(2)}) async-start(bf16[8,1024,256]{1,2,0:T(8,128)(2,1)} %pad_maximum_fusion), calls=%async_computation | async-start | bytes 8388608 | tf_op jit(solution)/shard_map/all_to_all | solution.py:45
  29.7 47.9 %all_gather.3 = bf16[128,2048]{1,0:T(8,128)(2,1)S(1)} all-gather(bf16[32,2048]{1,0:T(8,128)(2,1)S(1)} %all_to_all.28), channel_id=1, replica_groups=mesh['rh'=8,'rl'=4,'head'=8] {'rl'}, dimensions={0}, use_global_device_ids=true | all-gather | bytes 655360 | tf_op jit(solution)/shard_map/all_gather | solution.py:42
  78.5 6.5 %copy.69 = bf16[8,1024,2,1,128]{4,1,3,2,0:T(8,128)(2,1)} copy(bf16[8,1024,2,1,128]{1,4,2,0,3:T(8,128)(2,1)} %bitcast.20) | data formatting | bytes 8388608 | tf_op jit(solution)/shard_map/while | solution.py:104
  85.0 160.4 %while.14 = (s32[]{:T(128)}, f32[8,128,16,128]{1,3,2,0:T(8,128)}, f32[8,128,16]{1,2,0:T(8,128)S(1)}, s32[8]{0:T(128)S(1)}, bf16[8,1024,2,1,128]{4,1,3,2,0:T(8,12...) while((s32[]{:T(128)}, f32[8,128,16,128]{1,3,2,0:T(8,128)}, ...), condition=%wide.region_5.6_spmd, body=%wide.region_0.5_spmd.sunk | while | flops 1119164416 | bytes 55485768 | solution.py:104
  88.9 5.5 %bitcast_reduce_fusion.2 = (f32[128,16]{0,1:T(8,128)S(1)}, f32[1024,128,16]{1,0,2:T(8,128)}) fusion(pred[1024]{0:T(1024)(128)(4,1)S(1)} %add_compare_fusion.3, bf16[128,1,16,128]{3,0,2,1:T(8,128)(2,1)S(1)} %get-tuple-element.349, bf16[8,1024,2,1,128]{4,1,3,2,0:T(8,128)(2,1)} %get-tuple-element.346, s32[]{:T(128)S(6)} %select_n.118), kind=kOutput, calls=%fused_computation.1.clone.1 | convolution fusion | flops 543160320 | bytes 9184260 | tf_op jit(solution)/shard_map/while/body/eval_jaxpr/igqd,pgd->igqp/dot_general | solution.py:63
  95.2 5.8 %fusion.85 = f32[128,128,16]{1,0,2:T(8,128)S(1)} fusion(f32[1024,128,16]{1,0,2:T(8,128)} %get-tuple-element.304, f32[128,16]{0,1:T(8,128)S(1)} %max.47, pred[1024]{0:T(1024)(128)(4,1)S(1)} %add_compare_fusion.3, bf16[8,1024,2,1,128]{4,1,3,2,0:T(8,128)(2,1)} %get-tuple-element.346, s32[]{:T(128)S(6)} %select_n.118), kind=kOutput, calls=%fused_computation.8.clone.1 | convolution fusion | flops 547356672 | bytes 9709572 | tf_op jit(solution)/shard_map/while/body/eval_jaxpr/igqp,pgd->igqd/dot_general | solution.py:84
  101.0 2.5 fusion.86
  108.9 5.5 %bitcast_reduce_fusion.2 = (f32[128,16]{0,1:T(8,128)S(1)}, f32[1024,128,16]{1,0,2:T(8,128)}) fusion(pred[1024]{0:T(1024)(128)(4,1)S(1)} %add_compare_fusion.3, bf16[128,1,16,128]{3,0,2,1:T(8,128)(2,1)S(1)} %get-tuple-element.349, bf16[8,1024,2,1,128]{4,1,3,2,0:T(8,128)(2,1)} %get-tuple-element.346, s32[]{:T(128)S(6)} %select_n.118), kind=kOutput, calls=%fused_computation.1.clone.1 | convolution fusion | flops 543160320 | bytes 9184260 | tf_op jit(solution)/shard_map/while/body/eval_jaxpr/igqd,pgd->igqp/dot_general | solution.py:63
  115.2 5.8 %fusion.85 = f32[128,128,16]{1,0,2:T(8,128)S(1)} fusion(f32[1024,128,16]{1,0,2:T(8,128)} %get-tuple-element.304, f32[128,16]{0,1:T(8,128)S(1)} %max.47, pred[1024]{0:T(1024)(128)(4,1)S(1)} %add_compare_fusion.3, bf16[8,1024,2,1,128]{4,1,3,2,0:T(8,128)(2,1)} %get-tuple-element.346, s32[]{:T(128)S(6)} %select_n.118), kind=kOutput, calls=%fused_computation.8.clone.1 | convolution fusion | flops 547356672 | bytes 9709572 | tf_op jit(solution)/shard_map/while/body/eval_jaxpr/igqp,pgd->igqd/dot_general | solution.py:84
  121.1 2.5 fusion.86
  129.0 5.5 %bitcast_reduce_fusion.2 = (f32[128,16]{0,1:T(8,128)S(1)}, f32[1024,128,16]{1,0,2:T(8,128)}) fusion(pred[1024]{0:T(1024)(128)(4,1)S(1)} %add_compare_fusion.3, bf16[128,1,16,128]{3,0,2,1:T(8,128)(2,1)S(1)} %get-tuple-element.349, bf16[8,1024,2,1,128]{4,1,3,2,0:T(8,128)(2,1)} %get-tuple-element.346, s32[]{:T(128)S(6)} %select_n.118), kind=kOutput, calls=%fused_computation.1.clone.1 | convolution fusion | flops 543160320 | bytes 9184260 | tf_op jit(solution)/shard_map/while/body/eval_jaxpr/igqd,pgd->igqp/dot_general | solution.py:63
  135.3 5.8 %fusion.85 = f32[128,128,16]{1,0,2:T(8,128)S(1)} fusion(f32[1024,128,16]{1,0,2:T(8,128)} %get-tuple-element.304, f32[128,16]{0,1:T(8,128)S(1)} %max.47, pred[1024]{0:T(1024)(128)(4,1)S(1)} %add_compare_fusion.3, bf16[8,1024,2,1,128]{4,1,3,2,0:T(8,128)(2,1)} %get-tuple-element.346, s32[]{:T(128)S(6)} %select_n.118), kind=kOutput, calls=%fused_computation.8.clone.1 | convolution fusion | flops 547356672 | bytes 9709572 | tf_op jit(solution)/shard_map/while/body/eval_jaxpr/igqp,pgd->igqd/dot_general | solution.py:84
  141.2 2.5 fusion.86
  149.1 5.5 %bitcast_reduce_fusion.2 = (f32[128,16]{0,1:T(8,128)S(1)}, f32[1024,128,16]{1,0,2:T(8,128)}) fusion(pred[1024]{0:T(1024)(128)(4,1)S(1)} %add_compare_fusion.3, bf16[128,1,16,128]{3,0,2,1:T(8,128)(2,1)S(1)} %get-tuple-element.349, bf16[8,1024,2,1,128]{4,1,3,2,0:T(8,128)(2,1)} %get-tuple-element.346, s32[]{:T(128)S(6)} %select_n.118), kind=kOutput, calls=%fused_computation.1.clone.1 | convolution fusion | flops 543160320 | bytes 9184260 | tf_op jit(solution)/shard_map/while/body/eval_jaxpr/igqd,pgd->igqp/dot_general | solution.py:63
  155.3 5.8 %fusion.85 = f32[128,128,16]{1,0,2:T(8,128)S(1)} fusion(f32[1024,128,16]{1,0,2:T(8,128)} %get-tuple-element.304, f32[128,16]{0,1:T(8,128)S(1)} %max.47, pred[1024]{0:T(1024)(128)(4,1)S(1)} %add_compare_fusion.3, bf16[8,1024,2,1,128]{4,1,3,2,0:T(8,128)(2,1)} %get-tuple-element.346, s32[]{:T(128)S(6)} %select_n.118), kind=kOutput, calls=%fused_computation.8.clone.1 | convolution fusion | flops 547356672 | bytes 9709572 | tf_op jit(solution)/shard_map/while/body/eval_jaxpr/igqp,pgd->igqd/dot_general | solution.py:84
  161.2 2.5 fusion.86
  169.1 5.5 %bitcast_reduce_fusion.2 = (f32[128,16]{0,1:T(8,128)S(1)}, f32[1024,128,16]{1,0,2:T(8,128)}) fusion(pred[1024]{0:T(1024)(128)(4,1)S(1)} %add_compare_fusion.3, bf16[128,1,16,128]{3,0,2,1:T(8,128)(2,1)S(1)} %get-tuple-element.349, bf16[8,1024,2,1,128]{4,1,3,2,0:T(8,128)(2,1)} %get-tuple-element.346, s32[]{:T(128)S(6)} %select_n.118), kind=kOutput, calls=%fused_computation.1.clone.1 | convolution fusion | flops 543160320 | bytes 9184260 | tf_op jit(solution)/shard_map/while/body/eval_jaxpr/igqd,pgd->igqp/dot_general | solution.py:63
  175.4 5.8 %fusion.85 = f32[128,128,16]{1,0,2:T(8,128)S(1)} fusion(f32[1024,128,16]{1,0,2:T(8,128)} %get-tuple-element.304, f32[128,16]{0,1:T(8,128)S(1)} %max.47, pred[1024]{0:T(1024)(128)(4,1)S(1)} %add_compare_fusion.3, bf16[8,1024,2,1,128]{4,1,3,2,0:T(8,128)(2,1)} %get-tuple-element.346, s32[]{:T(128)S(6)} %select_n.118), kind=kOutput, calls=%fused_computation.8.clone.1 | convolution fusion | flops 547356672 | bytes 9709572 | tf_op jit(solution)/shard_map/while/body/eval_jaxpr/igqp,pgd->igqd/dot_general | solution.py:84
  181.2 2.5 fusion.86
  189.1 5.5 %bitcast_reduce_fusion.2 = (f32[128,16]{0,1:T(8,128)S(1)}, f32[1024,128,16]{1,0,2:T(8,128)}) fusion(pred[1024]{0:T(1024)(128)(4,1)S(1)} %add_compare_fusion.3, bf16[128,1,16,128]{3,0,2,1:T(8,128)(2,1)S(1)} %get-tuple-element.349, bf16[8,1024,2,1,128]{4,1,3,2,0:T(8,128)(2,1)} %get-tuple-element.346, s32[]{:T(128)S(6)} %select_n.118), kind=kOutput, calls=%fused_computation.1.clone.1 | convolution fusion | flops 543160320 | bytes 9184260 | tf_op jit(solution)/shard_map/while/body/eval_jaxpr/igqd,pgd->igqp/dot_general | solution.py:63
  195.4 5.8 %fusion.85 = f32[128,128,16]{1,0,2:T(8,128)S(1)} fusion(f32[1024,128,16]{1,0,2:T(8,128)} %get-tuple-element.304, f32[128,16]{0,1:T(8,128)S(1)} %max.47, pred[1024]{0:T(1024)(128)(4,1)S(1)} %add_compare_fusion.3, bf16[8,1024,2,1,128]{4,1,3,2,0:T(8,128)(2,1)} %get-tuple-element.346, s32[]{:T(128)S(6)} %select_n.118), kind=kOutput, calls=%fused_computation.8.clone.1 | convolution fusion | flops 547356672 | bytes 9709572 | tf_op jit(solution)/shard_map/while/body/eval_jaxpr/igqp,pgd->igqd/dot_general | solution.py:84
  209.2 5.5 %bitcast_reduce_fusion.2 = (f32[128,16]{0,1:T(8,128)S(1)}, f32[1024,128,16]{1,0,2:T(8,128)}) fusion(pred[1024]{0:T(1024)(128)(4,1)S(1)} %add_compare_fusion.3, bf16[128,1,16,128]{3,0,2,1:T(8,128)(2,1)S(1)} %get-tuple-element.349, bf16[8,1024,2,1,128]{4,1,3,2,0:T(8,128)(2,1)} %get-tuple-element.346, s32[]{:T(128)S(6)} %select_n.118), kind=kOutput, calls=%fused_computation.1.clone.1 | convolution fusion | flops 543160320 | bytes 9184260 | tf_op jit(solution)/shard_map/while/body/eval_jaxpr/igqd,pgd->igqp/dot_general | solution.py:63
  215.5 5.8 %fusion.85 = f32[128,128,16]{1,0,2:T(8,128)S(1)} fusion(f32[1024,128,16]{1,0,2:T(8,128)} %get-tuple-element.304, f32[128,16]{0,1:T(8,128)S(1)} %max.47, pred[1024]{0:T(1024)(128)(4,1)S(1)} %add_compare_fusion.3, bf16[8,1024,2,1,128]{4,1,3,2,0:T(8,128)(2,1)} %get-tuple-element.346, s32[]{:T(128)S(6)} %select_n.118), kind=kOutput, calls=%fused_computation.8.clone.1 | convolution fusion | flops 547356672 | bytes 9709572 | tf_op jit(solution)/shard_map/while/body/eval_jaxpr/igqp,pgd->igqd/dot_general | solution.py:84
  229.3 5.5 %bitcast_reduce_fusion.2 = (f32[128,16]{0,1:T(8,128)S(1)}, f32[1024,128,16]{1,0,2:T(8,128)}) fusion(pred[1024]{0:T(1024)(128)(4,1)S(1)} %add_compare_fusion.3, bf16[128,1,16,128]{3,0,2,1:T(8,128)(2,1)S(1)} %get-tuple-element.349, bf16[8,1024,2,1,128]{4,1,3,2,0:T(8,128)(2,1)} %get-tuple-element.346, s32[]{:T(128)S(6)} %select_n.118), kind=kOutput, calls=%fused_computation.1.clone.1 | convolution fusion | flops 543160320 | bytes 9184260 | tf_op jit(solution)/shard_map/while/body/eval_jaxpr/igqd,pgd->igqp/dot_general | solution.py:63
  235.5 5.8 %fusion.85 = f32[128,128,16]{1,0,2:T(8,128)S(1)} fusion(f32[1024,128,16]{1,0,2:T(8,128)} %get-tuple-element.304, f32[128,16]{0,1:T(8,128)S(1)} %max.47, pred[1024]{0:T(1024)(128)(4,1)S(1)} %add_compare_fusion.3, bf16[8,1024,2,1,128]{4,1,3,2,0:T(8,128)(2,1)} %get-tuple-element.346, s32[]{:T(128)S(6)} %select_n.118), kind=kOutput, calls=%fused_computation.8.clone.1 | convolution fusion | flops 547356672 | bytes 9709572 | tf_op jit(solution)/shard_map/while/body/eval_jaxpr/igqp,pgd->igqd/dot_general | solution.py:84
  245.5 4.8 %multiply_reduce_fusion = f32[128,16,128]{0,2,1:T(8,128)S(1)} fusion(f32[8,128,16,128]{1,3,2,0:T(8,128)} %get-tuple-element.146, f32[8,128,16]{1,2,0:T(8,128)S(1)} %get-tuple-element.224), kind=kLoop, calls=%fused_computation.46 | loop fusion | flops 3932160 | bytes 9502720 | tf_op jit(solution)/shard_map/reduce_sum | solution.py:108
  252.2 5.2 %all-to-all-start.2 = ((f32[4,32,2080]{2,1,0:T(8,128)}), f32[4,32,2080]{2,1,0:T(8,128)S(1)}, u32[]{:S(2)}, u32[]{:S(2)}) async-start(f32[4,32,2080]{2,1,0:T(8,128)} %concatenate.17), calls=%async_computation.2 | async-start | bytes 2228224 | tf_op jit(solution)/shard_map/all_to_all | solution.py:112
  258.7 13.1 %all-to-all-done.2 = f32[4,32,2080]{2,1,0:T(8,128)S(1)} async-done(((f32[4,32,2080]{2,1,0:T(8,128)}), f32[4,32,2080]{2,1,0:T(8,128)S(1)}, u32[]{:S(2)}, u32[]{:S(2)}) %all-to-all-start.2) | async-done | bytes 1064992 | tf_op jit(solution)/shard_map/all_to_all | solution.py:112
  (150 shorter events, 38.4 us)
Async XLA Ops:
  0.0 78.3 %copy-start = (bf16[32,128]{1,0:T(8,128)(2,1)S(1)}, bf16[32,128]{1,0:T(8,128)(2,1)}, u32[]{:S(2)}) copy-start(bf16[32,128]{1,0:T(8,128)(2,1)} %param.13) | copy-start | bytes 24580
  0.0 20.2 %all-to-all-start.1 = ((bf16[4,8,2048]{2,0,1:T(4,128)(2,1)}), bf16[4,8,2048]{2,0,1:T(4,128)(2,1)S(1)}, u32[]{:S(2)}, u32[]{:S(2)}) async-start(bf16[4,8,2048]{2,0,1:T(4,128)(2,1)} %bitcast.168), calls=%async_computation.1 | async-start | bytes 262144 | tf_op jit(solution)/shard_map/all_to_all | solution.py:41
  16.0 10.9 %copy-start.3 = (s32[8]{0:T(128)S(1)}, s32[8]{0:T(128)}, u32[]{:S(2)}) copy-start(s32[8]{0:T(128)} %param.17) | copy-start | bytes 100
  16.0 11.5 %copy-start.2 = (s32[8,128]{1,0:T(8,128)S(1)}, s32[8,128]{1,0:T(8,128)}, u32[]{:S(2)}) copy-start(s32[8,128]{1,0:T(8,128)} %param.15) | copy-start | bytes 12292
  20.2 58.3 %all-to-all-start = ((bf16[8,1024,256]{1,2,0:T(8,128)(2,1)}), bf16[8,1024,256]{1,2,0:T(8,128)(2,1)}, u32[]{:S(2)}, u32[]{:S(2)}) async-start(bf16[8,1024,256]{1,2,0:T(8,128)(2,1)} %pad_maximum_fusion), calls=%async_computation | async-start | bytes 8388608 | tf_op jit(solution)/shard_map/all_to_all | solution.py:45
  26.8 58.1 %copy-start.1 = (bf16[32,128]{1,0:T(8,128)(2,1)S(1)}, bf16[32,128]{1,0:T(8,128)(2,1)}, u32[]{:S(2)}) copy-start(bf16[32,128]{1,0:T(8,128)(2,1)} %param.14) | copy-start | bytes 24580
  95.1 5.9 %slice-start = ((s8[8388608]{0:T(1024)(128)(4,1)}), s8[4194304]{0:T(1024)(128)(4,1)S(1)}, s32[]{:S(2)}) async-start(s8[8388608]{0:T(1024)(128)(4,1)} %bitcast.160), calls=%async_computation.3 | async-start | bytes 8388608 | tf_op jit(solution)/shard_map/while
  95.2 5.9 %slice-start.1 = ((s8[8388608]{0:T(1024)(128)(4,1)}), s8[4194304]{0:T(1024)(128)(4,1)S(1)}, s32[]{:S(2)}) async-start(s8[8388608]{0:T(1024)(128)(4,1)} %bitcast.160), calls=%async_computation.4 | async-start | bytes 8388608 | tf_op jit(solution)/shard_map/while
  115.1 5.9 %slice-start = ((s8[8388608]{0:T(1024)(128)(4,1)}), s8[4194304]{0:T(1024)(128)(4,1)S(1)}, s32[]{:S(2)}) async-start(s8[8388608]{0:T(1024)(128)(4,1)} %bitcast.160), calls=%async_computation.3 | async-start | bytes 8388608 | tf_op jit(solution)/shard_map/while
  115.2 5.9 %slice-start.1 = ((s8[8388608]{0:T(1024)(128)(4,1)}), s8[4194304]{0:T(1024)(128)(4,1)S(1)}, s32[]{:S(2)}) async-start(s8[8388608]{0:T(1024)(128)(4,1)} %bitcast.160), calls=%async_computation.4 | async-start | bytes 8388608 | tf_op jit(solution)/shard_map/while
  135.2 5.9 %slice-start = ((s8[8388608]{0:T(1024)(128)(4,1)}), s8[4194304]{0:T(1024)(128)(4,1)S(1)}, s32[]{:S(2)}) async-start(s8[8388608]{0:T(1024)(128)(4,1)} %bitcast.160), calls=%async_computation.3 | async-start | bytes 8388608 | tf_op jit(solution)/shard_map/while
  135.3 5.9 %slice-start.1 = ((s8[8388608]{0:T(1024)(128)(4,1)}), s8[4194304]{0:T(1024)(128)(4,1)S(1)}, s32[]{:S(2)}) async-start(s8[8388608]{0:T(1024)(128)(4,1)} %bitcast.160), calls=%async_computation.4 | async-start | bytes 8388608 | tf_op jit(solution)/shard_map/while
  155.2 5.9 %slice-start = ((s8[8388608]{0:T(1024)(128)(4,1)}), s8[4194304]{0:T(1024)(128)(4,1)S(1)}, s32[]{:S(2)}) async-start(s8[8388608]{0:T(1024)(128)(4,1)} %bitcast.160), calls=%async_computation.3 | async-start | bytes 8388608 | tf_op jit(solution)/shard_map/while
  155.3 5.9 %slice-start.1 = ((s8[8388608]{0:T(1024)(128)(4,1)}), s8[4194304]{0:T(1024)(128)(4,1)S(1)}, s32[]{:S(2)}) async-start(s8[8388608]{0:T(1024)(128)(4,1)} %bitcast.160), calls=%async_computation.4 | async-start | bytes 8388608 | tf_op jit(solution)/shard_map/while
  175.3 5.9 %slice-start = ((s8[8388608]{0:T(1024)(128)(4,1)}), s8[4194304]{0:T(1024)(128)(4,1)S(1)}, s32[]{:S(2)}) async-start(s8[8388608]{0:T(1024)(128)(4,1)} %bitcast.160), calls=%async_computation.3 | async-start | bytes 8388608 | tf_op jit(solution)/shard_map/while
  175.4 5.9 %slice-start.1 = ((s8[8388608]{0:T(1024)(128)(4,1)}), s8[4194304]{0:T(1024)(128)(4,1)S(1)}, s32[]{:S(2)}) async-start(s8[8388608]{0:T(1024)(128)(4,1)} %bitcast.160), calls=%async_computation.4 | async-start | bytes 8388608 | tf_op jit(solution)/shard_map/while
  195.3 5.9 %slice-start = ((s8[8388608]{0:T(1024)(128)(4,1)}), s8[4194304]{0:T(1024)(128)(4,1)S(1)}, s32[]{:S(2)}) async-start(s8[8388608]{0:T(1024)(128)(4,1)} %bitcast.160), calls=%async_computation.3 | async-start | bytes 8388608 | tf_op jit(solution)/shard_map/while
  195.4 5.9 %slice-start.1 = ((s8[8388608]{0:T(1024)(128)(4,1)}), s8[4194304]{0:T(1024)(128)(4,1)S(1)}, s32[]{:S(2)}) async-start(s8[8388608]{0:T(1024)(128)(4,1)} %bitcast.160), calls=%async_computation.4 | async-start | bytes 8388608 | tf_op jit(solution)/shard_map/while
  215.4 5.9 %slice-start = ((s8[8388608]{0:T(1024)(128)(4,1)}), s8[4194304]{0:T(1024)(128)(4,1)S(1)}, s32[]{:S(2)}) async-start(s8[8388608]{0:T(1024)(128)(4,1)} %bitcast.160), calls=%async_computation.3 | async-start | bytes 8388608 | tf_op jit(solution)/shard_map/while
  215.5 5.9 %slice-start.1 = ((s8[8388608]{0:T(1024)(128)(4,1)}), s8[4194304]{0:T(1024)(128)(4,1)S(1)}, s32[]{:S(2)}) async-start(s8[8388608]{0:T(1024)(128)(4,1)} %bitcast.160), calls=%async_computation.4 | async-start | bytes 8388608 | tf_op jit(solution)/shard_map/while
  235.4 5.9 %slice-start = ((s8[8388608]{0:T(1024)(128)(4,1)}), s8[4194304]{0:T(1024)(128)(4,1)S(1)}, s32[]{:S(2)}) async-start(s8[8388608]{0:T(1024)(128)(4,1)} %bitcast.160), calls=%async_computation.3 | async-start | bytes 8388608 | tf_op jit(solution)/shard_map/while
  235.5 5.9 %slice-start.1 = ((s8[8388608]{0:T(1024)(128)(4,1)}), s8[4194304]{0:T(1024)(128)(4,1)S(1)}, s32[]{:S(2)}) async-start(s8[8388608]{0:T(1024)(128)(4,1)} %bitcast.160), calls=%async_computation.4 | async-start | bytes 8388608 | tf_op jit(solution)/shard_map/while
  245.5 11.9 %copy-start.4 = (s32[8]{0:T(128)S(1)}, s32[8]{0:T(128)}, u32[]{:S(2)}) copy-start(s32[8]{0:T(128)} %param.16) | copy-start | bytes 100
  252.2 19.5 %all-to-all-start.2 = ((f32[4,32,2080]{2,1,0:T(8,128)}), f32[4,32,2080]{2,1,0:T(8,128)S(1)}, u32[]{:S(2)}, u32[]{:S(2)}) async-start(f32[4,32,2080]{2,1,0:T(8,128)} %concatenate.17), calls=%async_computation.2 | async-start | bytes 2228224 | tf_op jit(solution)/shard_map/all_to_all | solution.py:112
where the time goes:
time: 275 us; the launch traced here: 273 us
  matrix products  103 us (37%)
  blocking collectives  47.9 us (17%)
  other arithmetic  36.8 us (13%)
  loops' own time  27.8 us (10%)
  local copies, waits for them, and re-layouts  23.5 us (9%)
  starting transfers between devices  21 us (8%)
  waiting for transfers between devices  13.1 us (5%)
    all_gather x1, blocking collectives, body(): query_block = lax.all_gather(by_head, 'rl', axis=0, tiled=True)  47.9 us
    dot_general x8, matrix products, one_group(): jnp.einsum('igqp,pgd->igqd', cache_weights.astype(jnp.bfloat16), block_va...  46.3 us
    dot_general x8, matrix products, one_group(): jnp.einsum('igqd,pgd->igqp', query_block, block_keys, preferred_element_t...  43.9 us
    another operation x1, loops' own time, body(): partials, log_totals = lax.map(one_group, jnp.arange(n_hi, dtype=jnp.int32))  27.8 us
    reduce_sum x16, other arithmetic, one_group(): totals = jnp.sum(cache_weights, axis=3) + jnp.sum(tree_weights, axis=3)  20.8 us
    all_to_all x1, waiting for transfers between devices, body(): lax.all_to_all(payload, 'rl', split_axis=0, concat_axis=0, tiled=True)  13.1 us
    dot_general x8, matrix products, one_group(): jnp.einsum('igqr,rgd->igqd', tree_weights.astype(jnp.bfloat16), local_tre...  10.8 us
    all_to_all x1, starting transfers between devices, body(): lax.all_to_all(queries, 'head', split_axis=1, concat_axis=0, tiled=True)  9.15 us
  transfers between devices with their start and end apart: 3, of which 1 were waited for; matrix products, arithmetic and copies ran while one was open for 6% of the time, Pallas kernels for 0%

commit v1 on v0

--- a/solution.py
+++ b/solution.py
@@ -39,7 +39,9 @@
     node_count = parents.shape[1]
     rows_owned = tree_keys.shape[0]
     by_head = lax.all_to_all(queries, "head", split_axis=1, concat_axis=0, tiled=True)
-    query_block = lax.all_gather(by_head, "rl", axis=0, tiled=True)
+    query_block = jnp.concatenate(
+        lax.all_to_all(jnp.stack([by_head] * lax.axis_size("rl")), "rl", 0, 0), axis=0
+    )
     query_block = query_block.reshape(node_count, kv_local, group_size, HD)
     both = jnp.concatenate([cache_keys, cache_values], axis=2)
     mine = lax.all_to_all(both, "rh", split_axis=0, concat_axis=1, tiled=True)[0]

time: 275 us -> 288 us (1.047)
  waiting for transfers between devices: 13.1 us -> 60.4 us
  blocking collectives: 47.9 us -> 16.9 us
  starting transfers between devices: 21 us -> 17 us
    all_gather x1 -> x0, blocking collectives: 47.9 us -> none  [body(): query_block = lax.all_gather(by_head, 'rl', axis=0, tiled=True)]
    all_to_all x1, waiting for transfers between devices: 0.01 us -> 47.4 us  [body(): lax.all_to_all(both, 'rh', split_axis=0, concat_axis=1, tiled=True)[0]]
    all_to_all x0 -> x1, blocking collectives: none -> 16.9 us  [body(): lax.all_to_all(queries, 'head', split_axis=1, concat_axis=0, tiled=True)]
    all_to_all x1, starting transfers between devices: 9.15 us -> 5.72 us  [body(): lax.all_to_all(jnp.stack([by_head] * lax.axis_size('rl')), 'rl', 0, 0)]
    unnamed x12 -> x13, local copies, waits for them, and re-layouts: 6.81 us -> 6.93 us
  transfers between devices with their start and end apart: 3 -> 3, of which waited for: 1 -> 2; matrix products, arithmetic and copies ran while one was open for 6% -> 5% of each run, Pallas kernels for 0% -> 0%
where the time goes in v1:
time: 288 us; the launch traced here: 286 us
  matrix products  103 us (36%)
  waiting for transfers between devices  60.4 us (21%)
  other arithmetic  36.8 us (13%)
  loops' own time  27.8 us (10%)
  local copies, waits for them, and re-layouts  24 us (8%)
  starting transfers between devices  17 us (6%)
  blocking collectives  16.9 us (6%)
    all_to_all x1, waiting for transfers between devices, body(): lax.all_to_all(both, 'rh', split_axis=0, concat_axis=1, tiled=True)[0]  47.4 us
    dot_general x8, matrix products, one_group(): jnp.einsum('igqp,pgd->igqd', cache_weights.astype(jnp.bfloat16), block_va...  46.3 us
    dot_general x8, matrix products, one_group(): jnp.einsum('igqd,pgd->igqp', query_block, block_keys, preferred_element_t...  43.9 us
    another operation x1, loops' own time, body(): partials, log_totals = lax.map(one_group, jnp.arange(n_hi, dtype=jnp.int32))  27.8 us
    reduce_sum x16, other arithmetic, one_group(): totals = jnp.sum(cache_weights, axis=3) + jnp.sum(tree_weights, axis=3)  20.8 us
    all_to_all x1, blocking collectives, body(): lax.all_to_all(queries, 'head', split_axis=1, concat_axis=0, tiled=True)  16.9 us
    all_to_all x1, waiting for transfers between devices, body(): lax.all_to_all(payload, 'rl', split_axis=0, concat_axis=0, tiled=True)  13.1 us
    dot_general x8, matrix products, one_group(): jnp.einsum('igqr,rgd->igqd', tree_weights.astype(jnp.bfloat16), local_tre...  10.8 us
  transfers between devices with their start and end apart: 3, of which 2 were waited for; matrix products, arithmetic and copies ran while one was open for 5% of the time, Pallas kernels for 0%

profile of v1, /device:TPU:1, one launch (start us, length us, event | category | flops | bytes accessed | tf_op | source)
XLA Modules:
  0.0 286.4 jit_solution(724290896041709014)
XLA Ops:
  0.0 16.9 %all_to_all.35 = bf16[4,8,2048]{2,0,1:T(4,128)(2,1)S(1)} all-to-all(bf16[4,8,2048]{2,0,1:T(4,128)(2,1)} %bitcast.174), channel_id=1, replica_groups=mesh['rh'=8,'rl'=4,'head'=8] {'head'}, dimensions={1} | all-to-all | bytes 262144 | tf_op jit(solution)/shard_map/all_to_all | solution.py:41
  17.8 5.7 %all-to-all-start.2 = ((bf16[4,32,2048]{2,1,0:T(8,128)(2,1)}), bf16[4,32,2048]{2,1,0:T(8,128)(2,1)S(1)}, u32[]{:S(2)}, u32[]{:S(2)}) async-start(bf16[4,32,2048]{2,1,0:T(8,128)(2,1)} %stack.10), calls=%async_computation.2 | async-start | bytes 1048576 | tf_op jit(solution)/shard_map/all_to_all | solution.py:43
  23.5 2.9 copy.56
  26.4 3.9 %copy.55 = bf16[8,1024,128]{1,2,0:T(8,128)(2,1)} copy(bf16[8,1024,128]{2,1,0:T(8,128)(2,1)} %param.11) | data formatting | bytes 4194304 | tf_op args[1]
  30.3 4.2 %pad_maximum_fusion = bf16[8,1024,256]{1,2,0:T(8,128)(2,1)} fusion(bf16[8,1024,128]{1,2,0:T(8,128)(2,1)S(1)} %copy.56, bf16[8,1024,128]{1,2,0:T(8,128)(2,1)} %copy.55), kind=kLoop, calls=%fused_computation.47 | loop fusion | flops 8388608 | bytes 8388608 | tf_op jit(solution)/shard_map/concatenate | solution.py:46
  34.6 6.7 %all-to-all-start = ((bf16[8,1024,256]{1,2,0:T(8,128)(2,1)}), bf16[8,1024,256]{1,2,0:T(8,128)(2,1)}, u32[]{:S(2)}, u32[]{:S(2)}) async-start(bf16[8,1024,256]{1,2,0:T(8,128)(2,1)} %pad_maximum_fusion), calls=%async_computation | async-start | bytes 8388608 | tf_op jit(solution)/shard_map/all_to_all | solution.py:47
  44.6 47.4 %all-to-all-done = bf16[8,1024,256]{1,2,0:T(8,128)(2,1)} async-done(((bf16[8,1024,256]{1,2,0:T(8,128)(2,1)}), bf16[8,1024,256]{1,2,0:T(8,128)(2,1)}, u32[]{:S(2)}, u32[]{:S(2)}) %all-to-all-start) | async-done | bytes 4194336 | tf_op jit(solution)/shard_map/all_to_all | solution.py:47
  92.0 6.4 %copy.61 = bf16[8,1024,2,1,128]{4,1,3,2,0:T(8,128)(2,1)} copy(bf16[8,1024,2,1,128]{1,4,2,0,3:T(8,128)(2,1)} %bitcast.20) | data formatting | bytes 8388608 | tf_op jit(solution)/shard_map/while | solution.py:106
  98.5 160.4 %while.14 = (s32[]{:T(128)}, f32[8,128,16,128]{1,3,2,0:T(8,128)}, f32[8,128,16]{1,2,0:T(8,128)S(1)}, s32[8]{0:T(128)S(1)}, bf16[8,1024,2,1,128]{4,1,3,2,0:T(8,12...) while((s32[]{:T(128)}, f32[8,128,16,128]{1,3,2,0:T(8,128)}, ...), condition=%wide.region_5.6_spmd, body=%wide.region_0.5_spmd.sunk | while | flops 1119164416 | bytes 55485768 | solution.py:106
  102.4 5.5 %bitcast_reduce_fusion.2 = (f32[128,16]{0,1:T(8,128)S(1)}, f32[1024,128,16]{1,0,2:T(8,128)}) fusion(pred[1024]{0:T(1024)(128)(4,1)S(1)} %add_compare_fusion.3, bf16[128,1,16,128]{3,0,2,1:T(8,128)(2,1)S(1)} %get-tuple-element.349, bf16[8,1024,2,1,128]{4,1,3,2,0:T(8,128)(2,1)} %get-tuple-element.346, s32[]{:T(128)S(6)} %select_n.118), kind=kOutput, calls=%fused_computation.1.clone.1 | convolution fusion | flops 543160320 | bytes 9184260 | tf_op jit(solution)/shard_map/while/body/eval_jaxpr/igqd,pgd->igqp/dot_general | solution.py:65
  108.7 5.8 %fusion.85 = f32[128,128,16]{1,0,2:T(8,128)S(1)} fusion(f32[1024,128,16]{1,0,2:T(8,128)} %get-tuple-element.304, f32[128,16]{0,1:T(8,128)S(1)} %max.47, pred[1024]{0:T(1024)(128)(4,1)S(1)} %add_compare_fusion.3, bf16[8,1024,2,1,128]{4,1,3,2,0:T(8,128)(2,1)} %get-tuple-element.346, s32[]{:T(128)S(6)} %select_n.118), kind=kOutput, calls=%fused_computation.8.clone.1 | convolution fusion | flops 547356672 | bytes 9709572 | tf_op jit(solution)/shard_map/while/body/eval_jaxpr/igqp,pgd->igqd/dot_general | solution.py:86
  114.5 2.5 fusion.86
  122.4 5.5 %bitcast_reduce_fusion.2 = (f32[128,16]{0,1:T(8,128)S(1)}, f32[1024,128,16]{1,0,2:T(8,128)}) fusion(pred[1024]{0:T(1024)(128)(4,1)S(1)} %add_compare_fusion.3, bf16[128,1,16,128]{3,0,2,1:T(8,128)(2,1)S(1)} %get-tuple-element.349, bf16[8,1024,2,1,128]{4,1,3,2,0:T(8,128)(2,1)} %get-tuple-element.346, s32[]{:T(128)S(6)} %select_n.118), kind=kOutput, calls=%fused_computation.1.clone.1 | convolution fusion | flops 543160320 | bytes 9184260 | tf_op jit(solution)/shard_map/while/body/eval_jaxpr/igqd,pgd->igqp/dot_general | solution.py:65
  128.7 5.8 %fusion.85 = f32[128,128,16]{1,0,2:T(8,128)S(1)} fusion(f32[1024,128,16]{1,0,2:T(8,128)} %get-tuple-element.304, f32[128,16]{0,1:T(8,128)S(1)} %max.47, pred[1024]{0:T(1024)(128)(4,1)S(1)} %add_compare_fusion.3, bf16[8,1024,2,1,128]{4,1,3,2,0:T(8,128)(2,1)} %get-tuple-element.346, s32[]{:T(128)S(6)} %select_n.118), kind=kOutput, calls=%fused_computation.8.clone.1 | convolution fusion | flops 547356672 | bytes 9709572 | tf_op jit(solution)/shard_map/while/body/eval_jaxpr/igqp,pgd->igqd/dot_general | solution.py:86
  134.6 2.5 fusion.86
  142.5 5.5 %bitcast_reduce_fusion.2 = (f32[128,16]{0,1:T(8,128)S(1)}, f32[1024,128,16]{1,0,2:T(8,128)}) fusion(pred[1024]{0:T(1024)(128)(4,1)S(1)} %add_compare_fusion.3, bf16[128,1,16,128]{3,0,2,1:T(8,128)(2,1)S(1)} %get-tuple-element.349, bf16[8,1024,2,1,128]{4,1,3,2,0:T(8,128)(2,1)} %get-tuple-element.346, s32[]{:T(128)S(6)} %select_n.118), kind=kOutput, calls=%fused_computation.1.clone.1 | convolution fusion | flops 543160320 | bytes 9184260 | tf_op jit(solution)/shard_map/while/body/eval_jaxpr/igqd,pgd->igqp/dot_general | solution.py:65
  148.8 5.8 %fusion.85 = f32[128,128,16]{1,0,2:T(8,128)S(1)} fusion(f32[1024,128,16]{1,0,2:T(8,128)} %get-tuple-element.304, f32[128,16]{0,1:T(8,128)S(1)} %max.47, pred[1024]{0:T(1024)(128)(4,1)S(1)} %add_compare_fusion.3, bf16[8,1024,2,1,128]{4,1,3,2,0:T(8,128)(2,1)} %get-tuple-element.346, s32[]{:T(128)S(6)} %select_n.118), kind=kOutput, calls=%fused_computation.8.clone.1 | convolution fusion | flops 547356672 | bytes 9709572 | tf_op jit(solution)/shard_map/while/body/eval_jaxpr/igqp,pgd->igqd/dot_general | solution.py:86
  154.7 2.5 fusion.86
  162.6 5.5 %bitcast_reduce_fusion.2 = (f32[128,16]{0,1:T(8,128)S(1)}, f32[1024,128,16]{1,0,2:T(8,128)}) fusion(pred[1024]{0:T(1024)(128)(4,1)S(1)} %add_compare_fusion.3, bf16[128,1,16,128]{3,0,2,1:T(8,128)(2,1)S(1)} %get-tuple-element.349, bf16[8,1024,2,1,128]{4,1,3,2,0:T(8,128)(2,1)} %get-tuple-element.346, s32[]{:T(128)S(6)} %select_n.118), kind=kOutput, calls=%fused_computation.1.clone.1 | convolution fusion | flops 543160320 | bytes 9184260 | tf_op jit(solution)/shard_map/while/body/eval_jaxpr/igqd,pgd->igqp/dot_general | solution.py:65
  168.8 5.8 %fusion.85 = f32[128,128,16]{1,0,2:T(8,128)S(1)} fusion(f32[1024,128,16]{1,0,2:T(8,128)} %get-tuple-element.304, f32[128,16]{0,1:T(8,128)S(1)} %max.47, pred[1024]{0:T(1024)(128)(4,1)S(1)} %add_compare_fusion.3, bf16[8,1024,2,1,128]{4,1,3,2,0:T(8,128)(2,1)} %get-tuple-element.346, s32[]{:T(128)S(6)} %select_n.118), kind=kOutput, calls=%fused_computation.8.clone.1 | convolution fusion | flops 547356672 | bytes 9709572 | tf_op jit(solution)/shard_map/while/body/eval_jaxpr/igqp,pgd->igqd/dot_general | solution.py:86
  174.7 2.5 fusion.86
  182.6 5.5 %bitcast_reduce_fusion.2 = (f32[128,16]{0,1:T(8,128)S(1)}, f32[1024,128,16]{1,0,2:T(8,128)}) fusion(pred[1024]{0:T(1024)(128)(4,1)S(1)} %add_compare_fusion.3, bf16[128,1,16,128]{3,0,2,1:T(8,128)(2,1)S(1)} %get-tuple-element.349, bf16[8,1024,2,1,128]{4,1,3,2,0:T(8,128)(2,1)} %get-tuple-element.346, s32[]{:T(128)S(6)} %select_n.118), kind=kOutput, calls=%fused_computation.1.clone.1 | convolution fusion | flops 543160320 | bytes 9184260 | tf_op jit(solution)/shard_map/while/body/eval_jaxpr/igqd,pgd->igqp/dot_general | solution.py:65
  188.9 5.8 %fusion.85 = f32[128,128,16]{1,0,2:T(8,128)S(1)} fusion(f32[1024,128,16]{1,0,2:T(8,128)} %get-tuple-element.304, f32[128,16]{0,1:T(8,128)S(1)} %max.47, pred[1024]{0:T(1024)(128)(4,1)S(1)} %add_compare_fusion.3, bf16[8,1024,2,1,128]{4,1,3,2,0:T(8,128)(2,1)} %get-tuple-element.346, s32[]{:T(128)S(6)} %select_n.118), kind=kOutput, calls=%fused_computation.8.clone.1 | convolution fusion | flops 547356672 | bytes 9709572 | tf_op jit(solution)/shard_map/while/body/eval_jaxpr/igqp,pgd->igqd/dot_general | solution.py:86
  202.6 5.5 %bitcast_reduce_fusion.2 = (f32[128,16]{0,1:T(8,128)S(1)}, f32[1024,128,16]{1,0,2:T(8,128)}) fusion(pred[1024]{0:T(1024)(128)(4,1)S(1)} %add_compare_fusion.3, bf16[128,1,16,128]{3,0,2,1:T(8,128)(2,1)S(1)} %get-tuple-element.349, bf16[8,1024,2,1,128]{4,1,3,2,0:T(8,128)(2,1)} %get-tuple-element.346, s32[]{:T(128)S(6)} %select_n.118), kind=kOutput, calls=%fused_computation.1.clone.1 | convolution fusion | flops 543160320 | bytes 9184260 | tf_op jit(solution)/shard_map/while/body/eval_jaxpr/igqd,pgd->igqp/dot_general | solution.py:65
  208.9 5.8 %fusion.85 = f32[128,128,16]{1,0,2:T(8,128)S(1)} fusion(f32[1024,128,16]{1,0,2:T(8,128)} %get-tuple-element.304, f32[128,16]{0,1:T(8,128)S(1)} %max.47, pred[1024]{0:T(1024)(128)(4,1)S(1)} %add_compare_fusion.3, bf16[8,1024,2,1,128]{4,1,3,2,0:T(8,128)(2,1)} %get-tuple-element.346, s32[]{:T(128)S(6)} %select_n.118), kind=kOutput, calls=%fused_computation.8.clone.1 | convolution fusion | flops 547356672 | bytes 9709572 | tf_op jit(solution)/shard_map/while/body/eval_jaxpr/igqp,pgd->igqd/dot_general | solution.py:86
  222.7 5.5 %bitcast_reduce_fusion.2 = (f32[128,16]{0,1:T(8,128)S(1)}, f32[1024,128,16]{1,0,2:T(8,128)}) fusion(pred[1024]{0:T(1024)(128)(4,1)S(1)} %add_compare_fusion.3, bf16[128,1,16,128]{3,0,2,1:T(8,128)(2,1)S(1)} %get-tuple-element.349, bf16[8,1024,2,1,128]{4,1,3,2,0:T(8,128)(2,1)} %get-tuple-element.346, s32[]{:T(128)S(6)} %select_n.118), kind=kOutput, calls=%fused_computation.1.clone.1 | convolution fusion | flops 543160320 | bytes 9184260 | tf_op jit(solution)/shard_map/while/body/eval_jaxpr/igqd,pgd->igqp/dot_general | solution.py:65
  229.0 5.8 %fusion.85 = f32[128,128,16]{1,0,2:T(8,128)S(1)} fusion(f32[1024,128,16]{1,0,2:T(8,128)} %get-tuple-element.304, f32[128,16]{0,1:T(8,128)S(1)} %max.47, pred[1024]{0:T(1024)(128)(4,1)S(1)} %add_compare_fusion.3, bf16[8,1024,2,1,128]{4,1,3,2,0:T(8,128)(2,1)} %get-tuple-element.346, s32[]{:T(128)S(6)} %select_n.118), kind=kOutput, calls=%fused_computation.8.clone.1 | convolution fusion | flops 547356672 | bytes 9709572 | tf_op jit(solution)/shard_map/while/body/eval_jaxpr/igqp,pgd->igqd/dot_general | solution.py:86
  242.8 5.5 %bitcast_reduce_fusion.2 = (f32[128,16]{0,1:T(8,128)S(1)}, f32[1024,128,16]{1,0,2:T(8,128)}) fusion(pred[1024]{0:T(1024)(128)(4,1)S(1)} %add_compare_fusion.3, bf16[128,1,16,128]{3,0,2,1:T(8,128)(2,1)S(1)} %get-tuple-element.349, bf16[8,1024,2,1,128]{4,1,3,2,0:T(8,128)(2,1)} %get-tuple-element.346, s32[]{:T(128)S(6)} %select_n.118), kind=kOutput, calls=%fused_computation.1.clone.1 | convolution fusion | flops 543160320 | bytes 9184260 | tf_op jit(solution)/shard_map/while/body/eval_jaxpr/igqd,pgd->igqp/dot_general | solution.py:65
  249.0 5.8 %fusion.85 = f32[128,128,16]{1,0,2:T(8,128)S(1)} fusion(f32[1024,128,16]{1,0,2:T(8,128)} %get-tuple-element.304, f32[128,16]{0,1:T(8,128)S(1)} %max.47, pred[1024]{0:T(1024)(128)(4,1)S(1)} %add_compare_fusion.3, bf16[8,1024,2,1,128]{4,1,3,2,0:T(8,128)(2,1)} %get-tuple-element.346, s32[]{:T(128)S(6)} %select_n.118), kind=kOutput, calls=%fused_computation.8.clone.1 | convolution fusion | flops 547356672 | bytes 9709572 | tf_op jit(solution)/shard_map/while/body/eval_jaxpr/igqp,pgd->igqd/dot_general | solution.py:86
  259.0 4.8 %multiply_reduce_fusion = f32[128,16,128]{0,2,1:T(8,128)S(1)} fusion(f32[8,128,16,128]{1,3,2,0:T(8,128)} %get-tuple-element.146, f32[8,128,16]{1,2,0:T(8,128)S(1)} %get-tuple-element.224), kind=kLoop, calls=%fused_computation.46 | loop fusion | flops 3932160 | bytes 9502720 | tf_op jit(solution)/shard_map/reduce_sum | solution.py:110
  265.7 4.7 %all-to-all-start.3 = ((f32[4,32,2080]{2,1,0:T(8,128)}), f32[4,32,2080]{2,1,0:T(8,128)S(1)}, u32[]{:S(2)}, u32[]{:S(2)}) async-start(f32[4,32,2080]{2,1,0:T(8,128)} %concatenate.17), calls=%async_computation.3 | async-start | bytes 2228224 | tf_op jit(solution)/shard_map/all_to_all | solution.py:114
  271.7 13.1 %all-to-all-done.3 = f32[4,32,2080]{2,1,0:T(8,128)S(1)} async-done(((f32[4,32,2080]{2,1,0:T(8,128)}), f32[4,32,2080]{2,1,0:T(8,128)S(1)}, u32[]{:S(2)}, u32[]{:S(2)}) %all-to-all-start.3) | async-done | bytes 1064992 | tf_op jit(solution)/shard_map/all_to_all | solution.py:114
  (151 shorter events, 41.6 us)
Async XLA Ops:
  0.0 44.4 %copy-start = (bf16[32,128]{1,0:T(8,128)(2,1)S(1)}, bf16[32,128]{1,0:T(8,128)(2,1)}, u32[]{:S(2)}) copy-start(bf16[32,128]{1,0:T(8,128)(2,1)} %param.13) | copy-start | bytes 24580
  17.8 16.8 %all-to-all-start.2 = ((bf16[4,32,2048]{2,1,0:T(8,128)(2,1)}), bf16[4,32,2048]{2,1,0:T(8,128)(2,1)S(1)}, u32[]{:S(2)}, u32[]{:S(2)}) async-start(bf16[4,32,2048]{2,1,0:T(8,128)(2,1)} %stack.10), calls=%async_computation.2 | async-start | bytes 1048576 | tf_op jit(solution)/shard_map/all_to_all | solution.py:43
  30.3 10.9 %copy-start.3 = (s32[8]{0:T(128)S(1)}, s32[8]{0:T(128)}, u32[]{:S(2)}) copy-start(s32[8]{0:T(128)} %param.17) | copy-start | bytes 100
  30.3 11.5 %copy-start.2 = (s32[8,128]{1,0:T(8,128)S(1)}, s32[8,128]{1,0:T(8,128)}, u32[]{:S(2)}) copy-start(s32[8,128]{1,0:T(8,128)} %param.15) | copy-start | bytes 12292
  34.6 57.5 %all-to-all-start = ((bf16[8,1024,256]{1,2,0:T(8,128)(2,1)}), bf16[8,1024,256]{1,2,0:T(8,128)(2,1)}, u32[]{:S(2)}, u32[]{:S(2)}) async-start(bf16[8,1024,256]{1,2,0:T(8,128)(2,1)} %pad_maximum_fusion), calls=%async_computation | async-start | bytes 8388608 | tf_op jit(solution)/shard_map/all_to_all | solution.py:47
  41.2 57.3 %copy-start.1 = (bf16[32,128]{1,0:T(8,128)(2,1)S(1)}, bf16[32,128]{1,0:T(8,128)(2,1)}, u32[]{:S(2)}) copy-start(bf16[32,128]{1,0:T(8,128)(2,1)} %param.14) | copy-start | bytes 24580
  108.6 5.9 %slice-start = ((s8[8388608]{0:T(1024)(128)(4,1)}), s8[4194304]{0:T(1024)(128)(4,1)S(1)}, s32[]{:S(2)}) async-start(s8[8388608]{0:T(1024)(128)(4,1)} %bitcast.165), calls=%async_computation.4 | async-start | bytes 8388608 | tf_op jit(solution)/shard_map/while
  108.7 5.9 %slice-start.1 = ((s8[8388608]{0:T(1024)(128)(4,1)}), s8[4194304]{0:T(1024)(128)(4,1)S(1)}, s32[]{:S(2)}) async-start(s8[8388608]{0:T(1024)(128)(4,1)} %bitcast.165), calls=%async_computation.5 | async-start | bytes 8388608 | tf_op jit(solution)/shard_map/while
  128.6 5.9 %slice-start = ((s8[8388608]{0:T(1024)(128)(4,1)}), s8[4194304]{0:T(1024)(128)(4,1)S(1)}, s32[]{:S(2)}) async-start(s8[8388608]{0:T(1024)(128)(4,1)} %bitcast.165), calls=%async_computation.4 | async-start | bytes 8388608 | tf_op jit(solution)/shard_map/while
  128.7 5.9 %slice-start.1 = ((s8[8388608]{0:T(1024)(128)(4,1)}), s8[4194304]{0:T(1024)(128)(4,1)S(1)}, s32[]{:S(2)}) async-start(s8[8388608]{0:T(1024)(128)(4,1)} %bitcast.165), calls=%async_computation.5 | async-start | bytes 8388608 | tf_op jit(solution)/shard_map/while
  148.7 5.9 %slice-start = ((s8[8388608]{0:T(1024)(128)(4,1)}), s8[4194304]{0:T(1024)(128)(4,1)S(1)}, s32[]{:S(2)}) async-start(s8[8388608]{0:T(1024)(128)(4,1)} %bitcast.165), calls=%async_computation.4 | async-start | bytes 8388608 | tf_op jit(solution)/shard_map/while
  148.8 5.9 %slice-start.1 = ((s8[8388608]{0:T(1024)(128)(4,1)}), s8[4194304]{0:T(1024)(128)(4,1)S(1)}, s32[]{:S(2)}) async-start(s8[8388608]{0:T(1024)(128)(4,1)} %bitcast.165), calls=%async_computation.5 | async-start | bytes 8388608 | tf_op jit(solution)/shard_map/while
  168.7 5.9 %slice-start = ((s8[8388608]{0:T(1024)(128)(4,1)}), s8[4194304]{0:T(1024)(128)(4,1)S(1)}, s32[]{:S(2)}) async-start(s8[8388608]{0:T(1024)(128)(4,1)} %bitcast.165), calls=%async_computation.4 | async-start | bytes 8388608 | tf_op jit(solution)/shard_map/while
  168.8 5.9 %slice-start.1 = ((s8[8388608]{0:T(1024)(128)(4,1)}), s8[4194304]{0:T(1024)(128)(4,1)S(1)}, s32[]{:S(2)}) async-start(s8[8388608]{0:T(1024)(128)(4,1)} %bitcast.165), calls=%async_computation.5 | async-start | bytes 8388608 | tf_op jit(solution)/shard_map/while
  188.8 5.9 %slice-start = ((s8[8388608]{0:T(1024)(128)(4,1)}), s8[4194304]{0:T(1024)(128)(4,1)S(1)}, s32[]{:S(2)}) async-start(s8[8388608]{0:T(1024)(128)(4,1)} %bitcast.165), calls=%async_computation.4 | async-start | bytes 8388608 | tf_op jit(solution)/shard_map/while
  188.9 5.9 %slice-start.1 = ((s8[8388608]{0:T(1024)(128)(4,1)}), s8[4194304]{0:T(1024)(128)(4,1)S(1)}, s32[]{:S(2)}) async-start(s8[8388608]{0:T(1024)(128)(4,1)} %bitcast.165), calls=%async_computation.5 | async-start | bytes 8388608 | tf_op jit(solution)/shard_map/while
  208.8 5.9 %slice-start = ((s8[8388608]{0:T(1024)(128)(4,1)}), s8[4194304]{0:T(1024)(128)(4,1)S(1)}, s32[]{:S(2)}) async-start(s8[8388608]{0:T(1024)(128)(4,1)} %bitcast.165), calls=%async_computation.4 | async-start | bytes 8388608 | tf_op jit(solution)/shard_map/while
  208.9 5.9 %slice-start.1 = ((s8[8388608]{0:T(1024)(128)(4,1)}), s8[4194304]{0:T(1024)(128)(4,1)S(1)}, s32[]{:S(2)}) async-start(s8[8388608]{0:T(1024)(128)(4,1)} %bitcast.165), calls=%async_computation.5 | async-start | bytes 8388608 | tf_op jit(solution)/shard_map/while
  228.9 5.9 %slice-start = ((s8[8388608]{0:T(1024)(128)(4,1)}), s8[4194304]{0:T(1024)(128)(4,1)S(1)}, s32[]{:S(2)}) async-start(s8[8388608]{0:T(1024)(128)(4,1)} %bitcast.165), calls=%async_computation.4 | async-start | bytes 8388608 | tf_op jit(solution)/shard_map/while
  229.0 5.9 %slice-start.1 = ((s8[8388608]{0:T(1024)(128)(4,1)}), s8[4194304]{0:T(1024)(128)(4,1)S(1)}, s32[]{:S(2)}) async-start(s8[8388608]{0:T(1024)(128)(4,1)} %bitcast.165), calls=%async_computation.5 | async-start | bytes 8388608 | tf_op jit(solution)/shard_map/while
  248.9 5.9 %slice-start = ((s8[8388608]{0:T(1024)(128)(4,1)}), s8[4194304]{0:T(1024)(128)(4,1)S(1)}, s32[]{:S(2)}) async-start(s8[8388608]{0:T(1024)(128)(4,1)} %bitcast.165), calls=%async_computation.4 | async-start | bytes 8388608 | tf_op jit(solution)/shard_map/while
  249.0 5.9 %slice-start.1 = ((s8[8388608]{0:T(1024)(128)(4,1)}), s8[4194304]{0:T(1024)(128)(4,1)S(1)}, s32[]{:S(2)}) async-start(s8[8388608]{0:T(1024)(128)(4,1)} %bitcast.165), calls=%async_computation.5 | async-start | bytes 8388608 | tf_op jit(solution)/shard_map/while
  259.0 11.4 %copy-start.4 = (s32[8]{0:T(128)S(1)}, s32[8]{0:T(128)}, u32[]{:S(2)}) copy-start(s32[8]{0:T(128)} %param.16) | copy-start | bytes 100
  265.7 19.0 %all-to-all-start.3 = ((f32[4,32,2080]{2,1,0:T(8,128)}), f32[4,32,2080]{2,1,0:T(8,128)S(1)}, u32[]{:S(2)}, u32[]{:S(2)}) async-start(f32[4,32,2080]{2,1,0:T(8,128)} %concatenate.17), calls=%async_computation.3 | async-start | bytes 2228224 | tf_op jit(solution)/shard_map/all_to_all | solution.py:114
